TPU v7x, 32 devices: a whole 2x2x4 slice. The times are simulated.
32 devices in a mesh: blk: 32 (over z, y, x, core), feat: 1.
Axes of the slice: x: 2, y: 2, z: 4, core: 2. Of those that a mesh axis runs over, the one named last changes fastest.
Arguments:
- activations: bfloat16 [5120, 4096], P('blk', 'feat'), may hold values from -6 to 6
- live_rows: int32 [32], replicated, may hold values from 1 to 160, as said below
- encoder_weight: bfloat16 [4096, 32768], P('feat', 'blk'), may hold values from -0.09375 to 0.09375
- encoder_bias: float32 [32768], P('blk'), may hold values from -3 to 3
- decoder_weight: bfloat16 [4, 1024, 32768], P(None, 'feat', 'blk'), may hold values from -0.09375 to 0.09375
- decoder_bias: float32 [32768], P('blk'), may hold values from -3 to 3
- targets: bfloat16 [640, 32768], P('feat', 'blk'), may hold values from -6 to 6
Outputs:
- reconstruction: float32 [640, 32768], P('feat', 'blk')
- decoder_grad: float32 [4, 1024, 32768], P(None, 'feat', 'blk')
Inputs may be any that keep to these rules, and one draw needn't show every extreme that they name: `live_rows`: live rows of a block of 160 slots are its first ones; some block is full.
All inputs are finite; a program needn't handle non-finite values.
Results may differ from a plain program's by a relative error of at most 0.015.
Values may be sent and summed in bfloat16 or wider, within the bound.
A program may use at most 128 MiB of HBM per device.

v0:
```python
import jax
import jax.numpy as jnp
from jax import lax
from jax.sharding import PartitionSpec as P

G = 8


def from_partner(shard, axis, distance):
    return lax.ppermute(shard, axis, [(i, i ^ 1 << distance) for i in range(lax.axis_size(axis))])


def group_rows(block, levels, position):
    for bit in range(levels):
        other = from_partner(block, "blk", bit)
        upper = position >> bit & 1 == 1
        block = jnp.where(
            upper, jnp.concatenate([other, block], 0), jnp.concatenate([block, other], 0)
        )
    return block


def per_device(
    activations, live_rows, encoder_weight, encoder_bias, decoder_weight, decoder_bias, targets
):
    owners = lax.axis_size("blk") // G
    levels = owners.bit_length() - 1
    shares = lax.axis_size("feat")
    position = lax.axis_index("blk")
    share_index = lax.axis_index("feat")
    group_index = position // owners
    tok_rows = activations.shape[0]
    counts = lax.dynamic_slice_in_dim(live_rows, group_index * owners, owners)
    positions = jnp.arange(tok_rows, dtype=jnp.int32)
    live_mask = (positions[None, :] < counts[:, None]).astype(jnp.float32).reshape(-1)
    gathered = group_rows(activations, levels, position)
    per_share = encoder_weight.shape[1] // shares
    bias_share = lax.dynamic_slice_in_dim(encoder_bias, share_index * per_share, per_share)
    columns = encoder_weight
    whole = lax.psum(
        lax.dot_general(
            columns, gathered, (((0,), (1,)), ((), ())), preferred_element_type=jnp.float32
        ).astype(jnp.bfloat16),
        "feat",
    ).astype(jnp.float32)
    preact = lax.dynamic_slice_in_dim(whole, share_index * per_share, per_share, 0)
    codes_by_feature = (jax.nn.relu(preact + bias_share[:, None]) * live_mask[None, :]).astype(
        jnp.bfloat16
    )
    codes_all = group_rows(codes_by_feature, levels, position)
    decoder_rows = decoder_weight.reshape(-1, decoder_weight.shape[2])
    block_rows = gathered.shape[0] // shares
    columns = codes_all
    summed = lax.psum_scatter(
        lax.dot_general(
            columns, decoder_rows, (((0,), (0,)), ((), ())), preferred_element_type=jnp.float32
        ).astype(jnp.bfloat16),
        "feat",
        scatter_dimension=0,
        tiled=True,
    ).astype(jnp.float32)
    rebuilt = summed + decoder_bias[None, :]
    mask_block = lax.dynamic_slice_in_dim(live_mask, share_index * block_rows, block_rows)
    residual = ((rebuilt - targets.astype(jnp.float32)) * mask_block[:, None]).astype(jnp.bfloat16)
    columns = codes_all
    gradient = jnp.dot(
        columns,
        lax.all_gather(residual, "feat", axis=0, tiled=True),
        preferred_element_type=jnp.float32,
    )
    return (rebuilt, gradient.reshape(decoder_weight.shape))


def solution(mesh):
    in_specs = (
        P("blk", "feat"),
        P(),
        P("feat", "blk"),
        P("blk"),
        P(None, "feat", "blk"),
        P("blk"),
        P("feat", "blk"),
    )
    out_specs = (P("feat", "blk"), P(None, "feat", "blk"))
    return jax.shard_map(
        per_device, mesh=mesh, in_specs=in_specs, out_specs=out_specs, check_vma=False
    )
```

profile of v0, /device:TPU:0, one launch (start us, length us, event | category | flops | bytes accessed | tf_op | source)
XLA Modules:
  0.0 164.7 jit_solution(6277128677237673560)
XLA Ops:
  0.6 0.6 collective-permute-start
  1.2 0.0 copy-start.3
  1.2 0.0 copy-start.1
  1.2 3.0 %collective-permute-done = bf16[160,4096]{1,0:T(8,128)(2,1)} collective-permute-done((bf16[160,4096]{1,0:T(8,128)(2,1)}, bf16[160,4096]{1,0:T(8,128)(2,1)}, u32[]{:S(2)}, u32[]{:S(2)}) %collective-permute-start) | collective-permute-done | bytes 1310752 | tf_op jit(solution)/shard_map/ppermute | solution.py:10
  4.2 3.1 %maximum_select_fusion.3 = bf16[320,4096]{1,0:T(8,128)(2,1)S(1)} fusion(bf16[160,4096]{1,0:T(8,128)(2,1)} %param.7, bf16[160,4096]{1,0:T(8,128)(2,1)} %collective-permute-done, pred[]{:T(512)S(6)} %eq.9), kind=kLoop, calls=%fused_computation.9 | loop fusion | flops 11796480 | bytes 5242881 | tf_op jit(solution)/shard_map/jit(_where)/select_n | solution.py:17
  7.3 2.9 %collective-permute-start.1 = (bf16[320,4096]{1,0:T(8,128)(2,1)S(1)}, bf16[320,4096]{1,0:T(8,128)(2,1)}, u32[]{:S(2)}, u32[]{:S(2)}) collective-permute-start(bf16[320,4096]{1,0:T(8,128)(2,1)S(1)} %maximum_select_fusion.3), channel_id=1, source_target_pairs={{0,2},{1,3},{2,0},{3,1},{4,6},{5,7},{6,4},{7,5},{8,10},{9,11},{10,... | collective-permute-start | bytes 7864328 | tf_op jit(solution)/shard_map/ppermute | solution.py:10
  10.2 0.0 copy-done.3
  10.2 0.1 dynamic_slice.2
  10.3 0.1 fusion.11
  10.4 0.1 reshape.48
  10.5 57.0 %collective-permute-done.1 = bf16[320,4096]{1,0:T(8,128)(2,1)} collective-permute-done((bf16[320,4096]{1,0:T(8,128)(2,1)S(1)}, bf16[320,4096]{1,0:T(8,128)(2,1)}, u32[]{:S(2)}, u32[]{:S(2)}) %collective-permute-start.1) | collective-permute-done | bytes 2621472 | tf_op jit(solution)/shard_map/ppermute | solution.py:10
  67.5 0.0 copy-done.1
  67.5 10.5 %fusion.9 = bf16[1024,640]{0,1:T(8,128)(2,1)S(1)} fusion(f32[640]{0:T(1024)S(1)} %reshape.48, f32[1024]{0:T(1024)S(1)} %copy-done.1, bf16[4096,1024]{1,0:T(8,128)(2,1)} %param.9, bf16[320,4096]{1,0:T(8,128)(2,1)S(1)} %maximum_select_fusion.3, bf16[320,4096]{1,0:T(8,128)(2,1)} %collective-permute-done.1, pred[]{:T(512)S(6)} %eq.8), kind=kOutput, calls=%fused_computation.17 | convolution fusion | flops 5396234240 | bytes 14948865 | tf_op jit(solution)/shard_map/dot_general | solution.py:41
  78.0 0.0 copy-start.2
  78.0 0.1 collective-permute-start.2
  78.1 3.0 %collective-permute-done.2 = bf16[1024,640]{0,1:T(8,128)(2,1)S(1)} collective-permute-done((bf16[1024,640]{0,1:T(8,128)(2,1)S(1)}, bf16[1024,640]{0,1:T(8,128)(2,1)S(1)}, u32[]{:S(2)}, u32[]{:S(2)}) %collective-permute-start.2) | collective-permute-done | bytes 1310752 | tf_op jit(solution)/shard_map/ppermute | solution.py:10
  81.2 1.0 maximum_select_fusion.4
  82.1 1.8 %collective-permute-start.3 = (bf16[2048,640]{0,1:T(8,128)(2,1)S(1)}, bf16[2048,640]{0,1:T(8,128)(2,1)S(1)}, u32[]{:S(2)}, u32[]{:S(2)}) collective-permute-start(bf16[2048,640]{0,1:T(8,128)(2,1)S(1)} %maximum_select_fusion.4), channel_id=1, source_target_pairs={{0,2},{1,3},{2,0},{3,1},{4,6},{5,7},{6,4},{7,5},{8,10},{9,11},{10,... | collective-permute-start | bytes 7864328 | tf_op jit(solution)/shard_map/ppermute | solution.py:10
  84.0 57.2 %collective-permute-done.3 = bf16[2048,640]{0,1:T(8,128)(2,1)S(1)} collective-permute-done((bf16[2048,640]{0,1:T(8,128)(2,1)S(1)}, bf16[2048,640]{0,1:T(8,128)(2,1)S(1)}, u32[]{:S(2)}, u32[]{:S(2)}) %collective-permute-start.3) | collective-permute-done | bytes 2621472 | tf_op jit(solution)/shard_map/ppermute | solution.py:10
  141.1 0.0 copy-done.2
  141.1 0.0 copy-start
  141.1 9.0 %convert_add_fusion = f32[640,1024]{1,0:T(8,128)S(1)} fusion(bf16[4096,1024]{1,0:T(8,128)(2,1)} %bitcast.6, f32[1024]{0:T(1024)S(1)} %copy-done.2, bf16[2048,640]{0,1:T(8,128)(2,1)S(1)} %maximum_select_fusion.4, bf16[2048,640]{0,1:T(8,128)(2,1)S(1)} %collective-permute-done.3, pred[]{:T(512)S(6)} %eq.8), kind=kOutput, calls=%fused_computation.13 | convolution fusion | flops 5394268160 | bytes 16257025 | tf_op jit(solution)/shard_map/dot_general | solution.py:55
  150.2 0.0 copy-done
  150.2 0.0 copy-start.4
  150.2 14.5 %fusion.8 = f32[4096,1024]{1,0:T(8,128)} fusion(f32[640,1024]{1,0:T(8,128)S(1)} %convert_add_fusion, bf16[640,1024]{1,0:T(8,128)(2,1)S(1)} %copy-done, f32[640]{0:T(1024)S(1)} %reshape.48, bf16[2048,640]{0,1:T(8,128)(2,1)S(1)} %maximum_select_fusion.4, bf16[2048,640]{0,1:T(8,128)(2,1)S(1)} %collective-permute-done.3, pred[]{:T(512)S(6)} %eq.8), kind=kOutput, calls=%fused_computation.16 | convolution fusion | flops 5394923520 | bytes 25954816 | tf_op jit(solution)/shard_map/dot_general | solution.py:66
  164.7 0.0 copy-done.4
Async XLA Ops:
  0.6 3.6 %collective-permute-start = (bf16[160,4096]{1,0:T(8,128)(2,1)}, bf16[160,4096]{1,0:T(8,128)(2,1)}, u32[]{:S(2)}, u32[]{:S(2)}) collective-permute-start(bf16[160,4096]{1,0:T(8,128)(2,1)} %param.7), channel_id=1, source_target_pairs={{0,1},{1,0},{2,3},{3,2},{4,5},{5,4},{6,7},{7,6},{8,9},{9,8},{10,11... | collective-permute-start | bytes 3932168 | tf_op jit(solution)/shard_map/ppermute | solution.py:10
  1.2 9.0 %copy-start.3 = (s32[32]{0:T(128)S(1)}, s32[32]{0:T(128)}, u32[]{:S(2)}) copy-start(s32[32]{0:T(128)} %param.8) | copy-start | bytes 388
  1.2 66.3 %copy-start.1 = (f32[1024]{0:T(1024)S(1)}, f32[1024]{0:T(1024)}, u32[]{:S(2)}) copy-start(f32[1024]{0:T(1024)} %param.10) | copy-start | bytes 12292
  7.3 60.2 %collective-permute-start.1 = (bf16[320,4096]{1,0:T(8,128)(2,1)S(1)}, bf16[320,4096]{1,0:T(8,128)(2,1)}, u32[]{:S(2)}, u32[]{:S(2)}) collective-permute-start(bf16[320,4096]{1,0:T(8,128)(2,1)S(1)} %maximum_select_fusion.3), channel_id=1, source_target_pairs={{0,2},{1,3},{2,0},{3,1},{4,6},{5,7},{6,4},{7,5},{8,10},{9,11},{10,... | collective-permute-start | bytes 7864328 | tf_op jit(solution)/shard_map/ppermute | solution.py:10
  78.0 63.1 %copy-start.2 = (f32[1024]{0:T(1024)S(1)}, f32[1024]{0:T(1024)}, u32[]{:S(2)}) copy-start(f32[1024]{0:T(1024)} %param.12) | copy-start | bytes 12292
  78.0 3.1 %collective-permute-start.2 = (bf16[1024,640]{0,1:T(8,128)(2,1)S(1)}, bf16[1024,640]{0,1:T(8,128)(2,1)S(1)}, u32[]{:S(2)}, u32[]{:S(2)}) collective-permute-start(bf16[1024,640]{0,1:T(8,128)(2,1)S(1)} %fusion.9), channel_id=1, source_target_pairs={{0,1},{1,0},{2,3},{3,2},{4,5},{5,4},{6,7},{7,6},{8,9},{9,8},{10,11... | collective-permute-start | bytes 3932168 | tf_op jit(solution)/shard_map/ppermute | solution.py:10
  82.1 59.0 %collective-permute-start.3 = (bf16[2048,640]{0,1:T(8,128)(2,1)S(1)}, bf16[2048,640]{0,1:T(8,128)(2,1)S(1)}, u32[]{:S(2)}, u32[]{:S(2)}) collective-permute-start(bf16[2048,640]{0,1:T(8,128)(2,1)S(1)} %maximum_select_fusion.4), channel_id=1, source_target_pairs={{0,2},{1,3},{2,0},{3,1},{4,6},{5,7},{6,4},{7,5},{8,10},{9,11},{10,... | collective-permute-start | bytes 7864328 | tf_op jit(solution)/shard_map/ppermute | solution.py:10
  141.1 9.1 %copy-start = (bf16[640,1024]{1,0:T(8,128)(2,1)S(1)}, bf16[640,1024]{1,0:T(8,128)(2,1)}, u32[]{:S(2)}) copy-start(bf16[640,1024]{1,0:T(8,128)(2,1)} %param.13) | copy-start | bytes 3932164
  150.2 14.5 %copy-start.4 = (f32[640,1024]{1,0:T(8,128)}, f32[640,1024]{1,0:T(8,128)S(1)}, u32[]{:S(2)}) copy-start(f32[640,1024]{1,0:T(8,128)S(1)} %convert_add_fusion) | copy-start | bytes 7864324
where the time goes:
time: 165 us
  waiting for transfers between devices  120 us (73%)
  matrix products  34.1 us (21%)
  starting transfers between devices  5.35 us (3%)
  other arithmetic  4.17 us (3%)
    ppermute x4, waiting for transfers between devices, from_partner(): lax.ppermute(shard, axis, [(i, i ^ 1 << distance) for i in range(lax.axis...  120 us
    dot_general x1, matrix products, per_device(): jnp.dot(columns, lax.all_gather(residual, 'feat', axis=0, tiled=True), pr...  14.5 us
    dot_general x1, matrix products, per_device(): lax.dot_general(columns, gathered, (((0,), (1,)), ((), ())), preferred_el...  10.5 us
    dot_general x1, matrix products, per_device(): lax.dot_general(columns, decoder_rows, (((0,), (0,)), ((), ())), preferre...  9.05 us
    ppermute x4, starting transfers between devices, from_partner(): lax.ppermute(shard, axis, [(i, i ^ 1 << distance) for i in range(lax.axis...  5.35 us
    select_n x2, other arithmetic, group_rows(): jnp.where(upper, jnp.concatenate([other, block], 0), jnp.concatenate([blo...  4.1 us
  transfers between devices with their start and end apart: 4, of which 4 were waited for; matrix products, arithmetic and copies ran while one was open for 0% of the time, Pallas kernels for 0%

commit v1 on v0

--- a/solution.py
+++ b/solution.py
@@ -1,9 +1,357 @@
+import functools
+
 import jax
 import jax.numpy as jnp
 from jax import lax
+from jax.experimental import pallas as pl
+from jax.experimental.pallas import tpu as pltpu
 from jax.sharding import PartitionSpec as P
 
 G = 8
+MESH = pl.DeviceIdType.MESH
+
+
+def gather_kernel(
+    pieces,
+    act_hbm,
+    live_ref,
+    enc_hbm,
+    bias_ref,
+    dec_hbm,
+    codes_hbm,
+    summed_hbm,
+    acts,
+    enc,
+    dec,
+    codes,
+    part,
+    summed,
+    load_sem,
+    s1_send,
+    s1_recv,
+    s2_send,
+    s2_recv,
+    s3_send,
+    s3_recv,
+    t1_send,
+    t1_recv,
+    t2_send,
+    t2_recv,
+    t3_send,
+    t3_recv,
+    out_sem,
+):
+    position = lax.axis_index("blk")
+    share = lax.axis_index("feat")
+    base = position // 4 * 4
+    me = position % 4
+    core = me % 2
+    home = me - core
+    away = 2 - home
+    twin = home + 1 - core
+    peer = away + core
+    peer_twin = away + 1 - core
+    on_chip = (base + twin, share)
+    across = (base + peer, share)
+
+    rows = acts.shape[1]
+    piece = rows // pieces
+    width = enc.shape[1]
+    tile = min(256, width)
+    tiles = width // tile
+
+    def at_piece(h):
+        return pl.ds(h * piece, piece)
+
+    load_act = pltpu.make_async_copy(act_hbm, acts.at[me], load_sem.at[0])
+    load_enc = pltpu.make_async_copy(enc_hbm, enc, load_sem.at[1])
+    load_dec = pltpu.make_async_copy(dec_hbm, dec, load_sem.at[2])
+    load_act.start()
+    load_enc.start()
+    load_dec.start()
+
+    barrier = pltpu.get_barrier_semaphore()
+    for neighbour in (on_chip, across):
+        pl.semaphore_signal(barrier, inc=1, device_id=neighbour, device_id_type=MESH)
+    pl.semaphore_wait(barrier, 2)
+
+    def remote(src, dst, send, recv, to):
+        return pltpu.make_async_remote_copy(
+            src_ref=src,
+            dst_ref=dst,
+            send_sem=send,
+            recv_sem=recv,
+            device_id=to,
+            device_id_type=MESH,
+        )
+
+    def s1(b):
+        return remote(act_hbm, acts.at[b], s1_send.at[0], s1_recv.at[0], on_chip)
+
+    def s2(b, h):
+        return remote(
+            act_hbm.at[at_piece(h)],
+            acts.at[b, at_piece(h)],
+            s2_send.at[h],
+            s2_recv.at[h],
+            across,
+        )
+
+    def s3(b, h):
+        ref = acts.at[b, at_piece(h)]
+        return remote(ref, ref, s3_send.at[h], s3_recv.at[h], on_chip)
+
+    def t1(f, b):
+        ref = codes.at[f, b]
+        return remote(ref, ref, t1_send.at[b], t1_recv.at[b], on_chip)
+
+    def t2(f, b, h):
+        ref = codes.at[f, b, at_piece(h)]
+        return remote(ref, ref, t2_send.at[b, h], t2_recv.at[b, h], across)
+
+    def t3(f, b, h):
+        ref = codes.at[f, b, at_piece(h)]
+        return remote(ref, ref, t3_send.at[b, h], t3_recv.at[b, h], on_chip)
+
+    for h in range(pieces):
+        s2(me, h).start()
+    s1(me).start()
+
+    def encode(b):
+        live = live_ref[base + b]
+        keep = lax.broadcasted_iota(jnp.int32, (rows, tile), 0) < live
+
+        def column(n, carry):
+            at = pl.ds(pl.multiple_of(n * tile, tile), tile)
+            product = jnp.dot(acts[b], enc[:, at], preferred_element_type=jnp.float32)
+            value = product.astype(jnp.bfloat16).astype(jnp.float32) + bias_ref[:, at]
+            value = jnp.where(keep, jnp.maximum(value, 0.0), 0.0)
+            codes[me, b, :, at] = value.astype(jnp.bfloat16)
+            return carry
+
+        lax.fori_loop(0, tiles, column, 0)
+
+    def product_of(fs, b, at, h=None):
+        total = None
+        for f in fs:
+            left = codes[f, b] if h is None else codes[f, b, at_piece(h)]
+            term = jnp.dot(left, dec[f, :, at], preferred_element_type=jnp.float32)
+            total = term if total is None else total + term
+        return total
+
+    def out_codes(b, h):
+        return pltpu.make_async_copy(
+            codes.at[:, b, at_piece(h)], codes_hbm.at[:, b, at_piece(h)], out_sem.at[0, b, h]
+        )
+
+    def out_summed(b, h):
+        return pltpu.make_async_copy(
+            summed.at[b, at_piece(h)], summed_hbm.at[b, at_piece(h)], out_sem.at[1, b, h]
+        )
+
+    load_act.wait()
+    load_enc.wait()
+    encode(me)
+    s1(twin).wait_recv()
+    t1(me, me).start()
+    encode(twin)
+    t1(me, twin).start()
+    for b in (home, home + 1):
+        for h in range(pieces):
+            t2(me, b, h).start()
+    t1(twin, home).wait_recv()
+    t1(twin, home + 1).wait_recv()
+    load_dec.wait()
+
+    def half(b, slot):
+        def column(n, carry):
+            at = pl.ds(pl.multiple_of(n * tile, tile), tile)
+            part[slot, :, at] = product_of((home, home + 1), b, at)
+            return carry
+
+        lax.fori_loop(0, tiles, column, 0)
+
+    def half_step(slot, carry):
+        half(home + slot, slot)
+        return carry
+
+    lax.fori_loop(0, 2, half_step, 0)
+
+    for h in range(pieces):
+        s2(peer, h).wait_recv()
+        s3(peer, h).start()
+    encode(peer)
+    t1(me, peer).start()
+    for h in range(pieces):
+        s3(peer_twin, h).wait_recv()
+    encode(peer_twin)
+    t1(me, peer_twin).start()
+    for b in (away, away + 1):
+        for h in range(pieces):
+            t2(me, b, h).start()
+    for b in (away, away + 1):
+        for h in range(pieces):
+            t2(peer, b, h).wait_recv()
+            t3(peer, b, h).start()
+    t1(twin, away).wait_recv()
+    t1(twin, away + 1).wait_recv()
+
+    def away_step(i, carry):
+        b = away + i
+        for h in range(pieces):
+            t3(peer_twin, b, h).wait_recv()
+            out_codes(b, h).start()
+
+        def column(n, inner):
+            at = pl.ds(pl.multiple_of(n * tile, tile), tile)
+            summed[b, :, at] = product_of((0, 1, 2, 3), b, at).astype(jnp.bfloat16)
+            return inner
+
+        lax.fori_loop(0, tiles, column, 0)
+        for h in range(pieces):
+            out_summed(b, h).start()
+        return carry
+
+    lax.fori_loop(0, 2, away_step, 0)
+
+    def home_step(i, carry):
+        b = home + i
+        for h in range(pieces):
+            t2(peer, b, h).wait_recv()
+            t3(peer, b, h).start()
+            t3(peer_twin, b, h).wait_recv()
+            out_codes(b, h).start()
+
+            def column(n, inner):
+                at = pl.ds(pl.multiple_of(n * tile, tile), tile)
+                total = part[i, at_piece(h), at] + product_of((away, away + 1), b, at, h)
+                summed[b, at_piece(h), at] = total.astype(jnp.bfloat16)
+                return inner
+
+            lax.fori_loop(0, tiles, column, 0)
+            out_summed(b, h).start()
+        return carry
+
+    lax.fori_loop(0, 2, home_step, 0)
+
+    s1(me).wait_send()
+    for h in range(pieces):
+        s2(me, h).wait_send()
+        s3(peer, h).wait_send()
+    for b in range(4):
+        t1(me, b).wait_send()
+        for h in range(pieces):
+            t2(me, b, h).wait_send()
+            t3(peer, b, h).wait_send()
+            out_codes(b, h).wait()
+            out_summed(b, h).wait()
+
+
+def gradient_kernel(
+    live_ref, codes_ref, summed_ref, bias_ref, targets_ref, grad_ref, rebuilt_hbm, residual, rebuilt, sem
+):
+    step = pl.program_id(0)
+    copy = pltpu.make_async_copy(rebuilt, rebuilt_hbm, sem)
+
+    @pl.when(step == 0)
+    def _():
+        base = lax.axis_index("blk") // 4 * 4
+        rows, width = summed_ref.shape[1:]
+        for b in range(4):
+            at = pl.ds(b * rows, rows)
+            whole = summed_ref[b].astype(jnp.float32) + bias_ref[...]
+            rebuilt[at, :] = whole
+            keep = lax.broadcasted_iota(jnp.int32, (rows, width), 0) < live_ref[base + b]
+            error = jnp.where(keep, whole - targets_ref[at, :].astype(jnp.float32), 0.0)
+            residual[at, :] = error.astype(jnp.bfloat16)
+        copy.start()
+
+    grad_ref[0] = lax.dot_general(
+        codes_ref[0], residual[...], (((0,), (0,)), ((), ())), preferred_element_type=jnp.float32
+    )
+
+    @pl.when(step == pl.num_programs(0) - 1)
+    def _():
+        copy.wait()
+
+
+def four_owners(
+    activations, live_rows, encoder_weight, encoder_bias, decoder_weight, decoder_bias, targets
+):
+    rows, depth = activations.shape
+    features = encoder_weight.shape[1]
+    width = decoder_weight.shape[2]
+    tokens = targets.shape[0]
+    pieces = 2 if rows % 32 == 0 else 1
+    any_space = pl.BlockSpec(memory_space=pl.ANY)
+    in_vmem = pl.BlockSpec(memory_space=pltpu.VMEM)
+    in_smem = pl.BlockSpec(memory_space=pltpu.SMEM)
+    dma = pltpu.SemaphoreType.DMA
+    bf16 = jnp.bfloat16
+    codes, summed = pl.pallas_call(
+        functools.partial(gather_kernel, pieces),
+        out_shape=(
+            jax.ShapeDtypeStruct((4, 4, rows, features), bf16),
+            jax.ShapeDtypeStruct((4, rows, width), bf16),
+        ),
+        in_specs=[any_space, in_smem, any_space, in_vmem, any_space],
+        out_specs=(any_space, any_space),
+        scratch_shapes=[
+            pltpu.VMEM((4, rows, depth), bf16),
+            pltpu.VMEM((depth, features), bf16),
+            pltpu.VMEM((4, features, width), bf16),
+            pltpu.VMEM((4, 4, rows, features), bf16),
+            pltpu.VMEM((2, rows, width), jnp.float32),
+            pltpu.VMEM((4, rows, width), bf16),
+            dma((3,)),
+            dma((1,)),
+            dma((1,)),
+            dma((pieces,)),
+            dma((pieces,)),
+            dma((pieces,)),
+            dma((pieces,)),
+            dma((4,)),
+            dma((4,)),
+            dma((4, pieces)),
+            dma((4, pieces)),
+            dma((4, pieces)),
+            dma((4, pieces)),
+            dma((2, 4, pieces)),
+        ],
+        compiler_params=pltpu.CompilerParams(
+            collective_id=0, has_side_effects=True, vmem_limit_bytes=60 * 1024 * 1024
+        ),
+        name="gather_codes",
+    )(activations, live_rows, encoder_weight, encoder_bias[None, :], decoder_weight)
+
+    span = min(512, features)
+    per = features // span
+    grad, rebuilt = pl.pallas_call(
+        gradient_kernel,
+        grid=(4 * per,),
+        out_shape=(
+            jax.ShapeDtypeStruct((4, features, width), jnp.float32),
+            jax.ShapeDtypeStruct((tokens, width), jnp.float32),
+        ),
+        in_specs=[
+            in_smem,
+            pl.BlockSpec((1, tokens, span), lambda i: (i // per, 0, i % per)),
+            in_vmem,
+            in_vmem,
+            in_vmem,
+        ],
+        out_specs=(pl.BlockSpec((1, span, width), lambda i: (i // per, i % per, 0)), any_space),
+        scratch_shapes=[
+            pltpu.VMEM((tokens, width), bf16),
+            pltpu.VMEM((tokens, width), jnp.float32),
+            dma(()),
+        ],
+        compiler_params=pltpu.CompilerParams(
+            dimension_semantics=("arbitrary",), vmem_limit_bytes=60 * 1024 * 1024
+        ),
+        name="gradient",
+    )(live_rows, codes.reshape(4, tokens, features), summed, decoder_bias[None, :], targets)
+    return rebuilt, grad
 
 
 def from_partner(shard, axis, distance):
@@ -20,7 +368,7 @@
     return block
 
 
-def per_device(
+def general(
     activations, live_rows, encoder_weight, encoder_bias, decoder_weight, decoder_bias, targets
 ):
     owners = lax.axis_size("blk") // G
@@ -82,6 +430,11 @@
         P("feat", "blk"),
     )
     out_specs = (P("feat", "blk"), P(None, "feat", "blk"))
+    fused = mesh.shape["blk"] // G == 4 and mesh.shape["feat"] == 1
     return jax.shard_map(
-        per_device, mesh=mesh, in_specs=in_specs, out_specs=out_specs, check_vma=False
+        four_owners if fused else general,
+        mesh=mesh,
+        in_specs=in_specs,
+        out_specs=out_specs,
+        check_vma=False,
     )

time: 165 us -> 80.1 us (0.49)
  waiting for transfers between devices: 120 us -> 0 us
  Pallas kernels: 0 us -> 78.9 us
  matrix products: 34.1 us -> 0 us
  starting transfers between devices: 5.35 us -> 0 us
  other arithmetic: 4.17 us -> 0 us
    ppermute x4 -> x0, waiting for transfers between devices: 120 us -> none  [from_partner(): lax.ppermute(shard, axis, [(i, i ^ 1 << distance) for i in range(lax.axis...]
    pallas_call x0 -> x2, Pallas kernels: none -> 78.9 us  [the longest x1 64.8 us: four_owners(): pl.pallas_call(functools.partial(gather_kernel, pieces), out_shape=(jax.S...]
    dot_general x3 -> x0, matrix products: 34.1 us -> none  [the longest x1 14.5 us: per_device(): jnp.dot(columns, lax.all_gather(residual, 'feat', axis=0, tiled=True), pr...]
    ppermute x4 -> x0, starting transfers between devices: 5.35 us -> none  [from_partner(): lax.ppermute(shard, axis, [(i, i ^ 1 << distance) for i in range(lax.axis...]
    select_n x2 -> x0, other arithmetic: 4.1 us -> none  [group_rows(): jnp.where(upper, jnp.concatenate([other, block], 0), jnp.concatenate([blo...]
  transfers between devices with their start and end apart: 4 -> 0, of which waited for: 4 -> 0; matrix products, arithmetic and copies ran while one was open for 0% -> 0% of each run, Pallas kernels for 0% -> 0%
where the time goes in v1:
time: 80.1 us; the launch traced here: 79.6 us
  Pallas kernels  78.9 us (99%)
    pallas_call x1, Pallas kernels, four_owners(): pl.pallas_call(functools.partial(gather_kernel, pieces), out_shape=(jax.S...  64.8 us
    pallas_call x1, Pallas kernels, four_owners(): pl.pallas_call(gradient_kernel, grid=(4 * per,), out_shape=(jax.ShapeDtyp...  14.1 us

profile of v1, /device:TPU:0, one launch (start us, length us, event | category | flops | bytes accessed | tf_op | source)
XLA Modules:
  0.0 79.6 jit_solution(12320552409794322922)
XLA Ops:
  0.6 64.8 %gather_codes.1 = (bf16[4,4,160,1024]{3,2,1,0:T(8,128)(2,1)}, bf16[4,160,1024]{2,1,0:T(8,128)(2,1)}) custom-call(bf16[160,4096]{1,0:T(8,128)(2,1)} %act_hbm.1, s32[32]{0:T(128)} %live_ref.3, bf16[4096,1024]{1,0:T(8,128)(2,1)} %enc_hbm.1, f32[1,1024]{1,0:T(1,128)} %bitcast.5, bf16[4,1024,1024]{2,1,0:T(8,128)(2,1)} %dec_hbm.1), custom_call_target="tpu_custom_call" | custom-call | tf_op jit(solution)/shard_map/gather_codes/pallas_call | solution.py:291
  65.5 14.1 %gradient.1 = (f32[4,1024,1024]{2,1,0:T(8,128)}, f32[640,1024]{1,0:T(8,128)}) custom-call(s32[32]{0:T(128)} %live_ref.3, bf16[4,640,1024]{2,1,0:T(8,128)(2,1)} %bitcast.3, bf16[4,160,1024]{2,1,0:T(8,128)(2,1)} %get-tuple-element.7.summed_ref, f32[1,1024]{1,0:T(1,128)} %bitcast.4, bf16[640,1024]{1,0:T(8,128)(2,1)} %targets_ref.1), custom_call_target="tpu_custom_call" | custom-call | tf_op jit(solution)/shard_map/gradient/pallas_call | solution.py:329

commit v2 on v1

--- a/solution.py
+++ b/solution.py
@@ -18,14 +18,18 @@
     enc_hbm,
     bias_ref,
     dec_hbm,
-    codes_hbm,
-    summed_hbm,
+    dec_bias_ref,
+    targets_hbm,
+    codes_out,
+    summed,
+    grad,
     acts,
     enc,
     dec,
     codes,
     part,
-    summed,
+    targets,
+    residual,
     load_sem,
     s1_send,
     s1_recv,
@@ -51,10 +55,10 @@
     twin = home + 1 - core
     peer = away + core
     peer_twin = away + 1 - core
+    rows = acts.shape[1]
     on_chip = (base + twin, share)
     across = (base + peer, share)
 
-    rows = acts.shape[1]
     piece = rows // pieces
     width = enc.shape[1]
     tile = min(256, width)
@@ -66,9 +70,13 @@
     load_act = pltpu.make_async_copy(act_hbm, acts.at[me], load_sem.at[0])
     load_enc = pltpu.make_async_copy(enc_hbm, enc, load_sem.at[1])
     load_dec = pltpu.make_async_copy(dec_hbm, dec, load_sem.at[2])
+    load_targets = pltpu.make_async_copy(
+        targets_hbm.at[pl.ds(pl.multiple_of(away * rows, 16), 2 * rows)], targets, load_sem.at[3]
+    )
     load_act.start()
     load_enc.start()
     load_dec.start()
+    load_targets.start()
 
     barrier = pltpu.get_barrier_semaphore()
     for neighbour in (on_chip, across):
@@ -139,14 +147,9 @@
             total = term if total is None else total + term
         return total
 
-    def out_codes(b, h):
+    def out_codes(i, h):
         return pltpu.make_async_copy(
-            codes.at[:, b, at_piece(h)], codes_hbm.at[:, b, at_piece(h)], out_sem.at[0, b, h]
-        )
-
-    def out_summed(b, h):
-        return pltpu.make_async_copy(
-            summed.at[b, at_piece(h)], summed_hbm.at[b, at_piece(h)], out_sem.at[1, b, h]
+            codes.at[:, home + i, at_piece(h)], codes_out.at[:, i, at_piece(h)], out_sem.at[i, h]
         )
 
     load_act.wait()
@@ -200,19 +203,34 @@
         b = away + i
         for h in range(pieces):
             t3(peer_twin, b, h).wait_recv()
-            out_codes(b, h).start()
+        keep = lax.broadcasted_iota(jnp.int32, (rows, tile), 0) < live_ref[base + b]
+        here = pl.ds(pl.multiple_of(i * rows, 16), rows)
 
         def column(n, inner):
             at = pl.ds(pl.multiple_of(n * tile, tile), tile)
-            summed[b, :, at] = product_of((0, 1, 2, 3), b, at).astype(jnp.bfloat16)
+            rounded = product_of((0, 1, 2, 3), b, at).astype(jnp.bfloat16)
+            summed[b, :, at] = rounded
+            whole = rounded.astype(jnp.float32) + dec_bias_ref[:, at]
+            error = jnp.where(keep, whole - targets[here, at].astype(jnp.float32), 0.0)
+            residual[here, at] = error.astype(jnp.bfloat16)
             return inner
 
         lax.fori_loop(0, tiles, column, 0)
-        for h in range(pieces):
-            out_summed(b, h).start()
         return carry
 
+    load_targets.wait()
     lax.fori_loop(0, 2, away_step, 0)
+
+    def gradient_step(k, carry):
+        f = k // tiles
+        at = pl.ds(pl.multiple_of(k % tiles * tile, tile), tile)
+        left = codes[f, pl.ds(away, 2), :, at].reshape(2 * rows, tile)
+        grad[f, at, :] = lax.dot_general(
+            left, residual[...], (((0,), (0,)), ((), ())), preferred_element_type=jnp.float32
+        )
+        return carry
+
+    lax.fori_loop(0, 4 * tiles, gradient_step, 0)
 
     def home_step(i, carry):
         b = home + i
@@ -220,7 +238,7 @@
             t2(peer, b, h).wait_recv()
             t3(peer, b, h).start()
             t3(peer_twin, b, h).wait_recv()
-            out_codes(b, h).start()
+            out_codes(i, h).start()
 
             def column(n, inner):
                 at = pl.ds(pl.multiple_of(n * tile, tile), tile)
@@ -229,7 +247,6 @@
                 return inner
 
             lax.fori_loop(0, tiles, column, 0)
-            out_summed(b, h).start()
         return carry
 
     lax.fori_loop(0, 2, home_step, 0)
@@ -243,31 +260,49 @@
         for h in range(pieces):
             t2(me, b, h).wait_send()
             t3(peer, b, h).wait_send()
-            out_codes(b, h).wait()
-            out_summed(b, h).wait()
+    for i in range(2):
+        for h in range(pieces):
+            out_codes(i, h).wait()
 
 
 def gradient_kernel(
-    live_ref, codes_ref, summed_ref, bias_ref, targets_ref, grad_ref, rebuilt_hbm, residual, rebuilt, sem
+    live_ref,
+    codes_ref,
+    summed_ref,
+    bias_ref,
+    targets_ref,
+    part_ref,
+    grad_ref,
+    rebuilt_hbm,
+    residual,
+    rebuilt,
+    sem,
 ):
     step = pl.program_id(0)
     copy = pltpu.make_async_copy(rebuilt, rebuilt_hbm, sem)
+    span = grad_ref.shape[1]
+    per = part_ref.shape[1] // span
 
     @pl.when(step == 0)
     def _():
-        base = lax.axis_index("blk") // 4 * 4
+        position = lax.axis_index("blk")
+        base = position // 4 * 4
+        home = position % 4 // 2 * 2
         rows, width = summed_ref.shape[1:]
+        for i in range(2):
+            b = home + i
+            whole = summed_ref[b].astype(jnp.float32) + bias_ref[...]
+            keep = lax.broadcasted_iota(jnp.int32, (rows, width), 0) < live_ref[base + b]
+            wanted = targets_ref[pl.ds(pl.multiple_of(b * rows, 16), rows), :]
+            error = jnp.where(keep, whole - wanted.astype(jnp.float32), 0.0)
+            residual[pl.ds(i * rows, rows), :] = error.astype(jnp.bfloat16)
         for b in range(4):
-            at = pl.ds(b * rows, rows)
-            whole = summed_ref[b].astype(jnp.float32) + bias_ref[...]
-            rebuilt[at, :] = whole
-            keep = lax.broadcasted_iota(jnp.int32, (rows, width), 0) < live_ref[base + b]
-            error = jnp.where(keep, whole - targets_ref[at, :].astype(jnp.float32), 0.0)
-            residual[at, :] = error.astype(jnp.bfloat16)
+            rebuilt[pl.ds(b * rows, rows), :] = summed_ref[b].astype(jnp.float32) + bias_ref[...]
         copy.start()
 
-    grad_ref[0] = lax.dot_general(
-        codes_ref[0], residual[...], (((0,), (0,)), ((), ())), preferred_element_type=jnp.float32
+    at = pl.ds(pl.multiple_of(step % per * span, span), span)
+    grad_ref[0] = part_ref[step // per, at, :] + lax.dot_general(
+        codes_ref[step // per, :, at], residual[...], (((0,), (0,)), ((), ())), preferred_element_type=jnp.float32
     )
 
     @pl.when(step == pl.num_programs(0) - 1)
@@ -288,22 +323,24 @@
     in_smem = pl.BlockSpec(memory_space=pltpu.SMEM)
     dma = pltpu.SemaphoreType.DMA
     bf16 = jnp.bfloat16
-    codes, summed = pl.pallas_call(
+    codes, summed, part = pl.pallas_call(
         functools.partial(gather_kernel, pieces),
         out_shape=(
-            jax.ShapeDtypeStruct((4, 4, rows, features), bf16),
-            jax.ShapeDtypeStruct((4, rows, width), bf16),
+            pltpu.VMEM((4, 2, rows, features), bf16),
+            pltpu.VMEM((4, rows, width), bf16),
+            pltpu.VMEM((4, features, width), jnp.float32),
         ),
-        in_specs=[any_space, in_smem, any_space, in_vmem, any_space],
-        out_specs=(any_space, any_space),
+        in_specs=[any_space, in_smem, any_space, in_vmem, any_space, in_vmem, any_space],
+        out_specs=(in_vmem, in_vmem, in_vmem),
         scratch_shapes=[
             pltpu.VMEM((4, rows, depth), bf16),
             pltpu.VMEM((depth, features), bf16),
             pltpu.VMEM((4, features, width), bf16),
             pltpu.VMEM((4, 4, rows, features), bf16),
             pltpu.VMEM((2, rows, width), jnp.float32),
-            pltpu.VMEM((4, rows, width), bf16),
-            dma((3,)),
+            pltpu.VMEM((2 * rows, width), bf16),
+            pltpu.VMEM((2 * rows, width), bf16),
+            dma((4,)),
             dma((1,)),
             dma((1,)),
             dma((pieces,)),
@@ -316,13 +353,13 @@
             dma((4, pieces)),
             dma((4, pieces)),
             dma((4, pieces)),
-            dma((2, 4, pieces)),
+            dma((2, pieces)),
         ],
         compiler_params=pltpu.CompilerParams(
-            collective_id=0, has_side_effects=True, vmem_limit_bytes=60 * 1024 * 1024
+            collective_id=0, has_side_effects=True, vmem_limit_bytes=38 * 1024 * 1024
         ),
         name="gather_codes",
-    )(activations, live_rows, encoder_weight, encoder_bias[None, :], decoder_weight)
+    )(activations, live_rows, encoder_weight, encoder_bias[None, :], decoder_weight, decoder_bias[None, :], targets)
 
     span = min(512, features)
     per = features // span
@@ -335,22 +372,23 @@
         ),
         in_specs=[
             in_smem,
-            pl.BlockSpec((1, tokens, span), lambda i: (i // per, 0, i % per)),
+            in_vmem,
+            in_vmem,
             in_vmem,
             in_vmem,
             in_vmem,
         ],
         out_specs=(pl.BlockSpec((1, span, width), lambda i: (i // per, i % per, 0)), any_space),
         scratch_shapes=[
-            pltpu.VMEM((tokens, width), bf16),
+            pltpu.VMEM((2 * rows, width), bf16),
             pltpu.VMEM((tokens, width), jnp.float32),
             dma(()),
         ],
         compiler_params=pltpu.CompilerParams(
-            dimension_semantics=("arbitrary",), vmem_limit_bytes=60 * 1024 * 1024
+            dimension_semantics=("arbitrary",), vmem_limit_bytes=24 * 1024 * 1024
         ),
         name="gradient",
-    )(live_rows, codes.reshape(4, tokens, features), summed, decoder_bias[None, :], targets)
+    )(live_rows, codes.reshape(4, 2 * rows, features), summed, decoder_bias[None, :], targets, part)
     return rebuilt, grad
 
 

time: 80.1 us -> 81.6 us (1.019)
  Pallas kernels: 78.9 us -> 80.7 us
    pallas_call x1, Pallas kernels: 64.8 us -> 70.6 us  [four_owners(): pl.pallas_call(functools.partial(gather_kernel, pieces), out_shape=(pltpu...]
    pallas_call x1, Pallas kernels: 14.1 us -> 10.1 us  [four_owners(): pl.pallas_call(gradient_kernel, grid=(4 * per,), out_shape=(jax.ShapeDtyp...]
where the time goes in v2:
time: 81.6 us; the launch traced here: 81.4 us
  Pallas kernels  80.7 us (99%)
    pallas_call x1, Pallas kernels, four_owners(): pl.pallas_call(functools.partial(gather_kernel, pieces), out_shape=(pltpu...  70.6 us
    pallas_call x1, Pallas kernels, four_owners(): pl.pallas_call(gradient_kernel, grid=(4 * per,), out_shape=(jax.ShapeDtyp...  10.1 us

profile of v2, /device:TPU:0, one launch (start us, length us, event | category | flops | bytes accessed | tf_op | source)
XLA Modules:
  0.0 81.4 jit_solution(2368616456698697920)
XLA Ops:
  0.6 0.0 copy-start
  0.6 0.0 copy-start.1
  0.7 0.0 copy-start.2
  0.7 70.6 %gather_codes.1 = (bf16[4,2,160,1024]{3,2,1,0:T(8,128)(2,1)S(1)}, bf16[4,160,1024]{2,1,0:T(8,128)(2,1)S(1)}, f32[4,1024,1024]{2,1,0:T(8,128)S(1)}) custom-call(bf16[160,4096]{1,0:T(8,128)(2,1)} %act_hbm.1, s32[32]{0:T(128)} %live_ref.3, bf16[4096,1024]{1,0:T(8,128)(2,1)} %enc_hbm.1, f32[1,1024]{1,0:T(1,128)} %bitcast.6, bf16[4,1024,1024]{2,1,0:T(8,128)(2,1)} %dec_hbm.1, ...), custom_call_target="tpu_custom_call" | custom-call | tf_op jit(solution)/shard_map/gather_codes/pallas_call | solution.py:326
  71.3 0.0 copy-done
  71.3 0.0 copy-done.1
  71.3 0.0 copy-done.2
  71.3 10.1 %gradient.1 = (f32[4,1024,1024]{2,1,0:T(8,128)}, f32[640,1024]{1,0:T(8,128)}) custom-call(s32[32]{0:T(128)S(1)} %copy-done.2, bf16[4,320,1024]{2,1,0:T(8,128)(2,1)S(1)} %bitcast.3, bf16[4,160,1024]{2,1,0:T(8,128)(2,1)S(1)} %get-tuple-element.8.summed_ref, f32[1,1024]{1,0:T(1,128)S(1)} %bitcast.5, bf16[640,1024]{1,0:T(8,128)(2,1)S(1)} %copy-done, ...), custom_call_target="tpu_custom_call" | custom-call | tf_op jit(solution)/shard_map/gradient/pallas_call | solution.py:366
Async XLA Ops:
  0.6 70.7 %copy-start = (bf16[640,1024]{1,0:T(8,128)(2,1)S(1)}, bf16[640,1024]{1,0:T(8,128)(2,1)}, u32[]{:S(2)}) copy-start(bf16[640,1024]{1,0:T(8,128)(2,1)} %targets_ref.1) | copy-start | bytes 3932164
  0.6 70.7 %copy-start.1 = (f32[1024]{0:T(1024)S(1)}, f32[1024]{0:T(1024)}, u32[]{:S(2)}) copy-start(f32[1024]{0:T(1024)} %param.12) | copy-start | bytes 12292
  0.7 70.7 %copy-start.2 = (s32[32]{0:T(128)S(1)}, s32[32]{0:T(128)}, u32[]{:S(2)}) copy-start(s32[32]{0:T(128)} %live_ref.3) | copy-start | bytes 388
